TPU v7x, 32 devices: a whole 2x2x4 slice. The times are simulated.
32 devices in a mesh: seq: 16 (over z, y, x), col: 2 (over core).
Axes of the slice: x: 2, y: 2, z: 4, core: 2. Of those that a mesh axis runs over, the one named last changes fastest.
Arguments:
- hidden: bfloat16 [4, 96, 2304], P(None, None, 'seq'), may hold values from -6 to 6
- key_cache: bfloat16 [1152, 128, 2048], P('seq', None, 'col'), may hold values from -300 to 300
- value_cache: bfloat16 [1152, 128, 2048], P('seq', None, 'col'), may hold values from -6 to 6
- page_table: int32 [96, 128], replicated, may hold values from 0 to 1151, as said below
- cache_len: int32 [96], replicated, may hold values from 1 to 16380, as said below
- order: int32 [96], replicated, may hold values from 0 to 95, each once
- route_ids: int32 [4, 96, 2], replicated, may hold values from 0 to 7, all different within a row; in each aligned block of 96 rows (0 to 95, 96 to 191, ..., all dimensions but the last counted through in order) at most 48 rows name the same one
- w_qkv: bfloat16 [2304, 3, 2048], P('seq', None, 'col'), may hold values from -0.125 to 0.125
- w_out: bfloat16 [2048, 2304], P('col', 'seq'), may hold values from -0.125 to 0.125
- w_router: bfloat16 [2304, 8], replicated, may hold values from -0.125 to 0.125
- w_gate_up: bfloat16 [8, 2304, 2, 5760], P('col', None, None, 'seq'), may hold values from -0.125 to 0.125
- w_down: bfloat16 [8, 5760, 2304], P('col', 'seq'), may hold values from -0.109375 to 0.109375
Outputs:
- layer_out: bfloat16 [4, 96, 2304], P(None, None, 'seq')
- new_keys: bfloat16 [4, 96, 2048], P(None, None, 'col')
- new_values: bfloat16 [4, 96, 2048], P(None, None, 'col')
Inputs may be any that keep to these rules, and one draw needn't show every extreme that they name: `cache_len`: one request's cache holds exactly 16380 tokens; 4 requests hold more than 640 tokens, the others at most 640. `page_table`: for request r the entries 0 to ceil((cache_len[r] + 4) / 128) - 1 name pages that no other such entry names; later entries are never read. `order`: each request sits in exactly one batch slot. `route_ids`: the two experts of a row differ; in each step no expert is named by more than 48 requests.
All inputs are finite; a program needn't handle non-finite values.
Results may differ from a plain program's by a relative error of at most 0.011.
Values may be sent and summed in bfloat16 or wider, within the bound.
A program may use at most 256 MiB of HBM per device.

v0:
```python
import jax
import jax.numpy as jnp
from jax import lax
from jax.sharding import PartitionSpec as P

HEAD_DIM = 64


EPSILON = 1e-05
LOWEST = -1e30


def rotate(row_data, positions, head_dim):
    head_count = row_data.shape[1] // head_dim
    half_dim = head_dim // 2
    frequency = jnp.exp(
        -jnp.log(10000.0) * 2.0 * jnp.arange(half_dim, dtype=jnp.float32) / head_dim
    )
    angles = positions.astype(jnp.float32)[:, None] * frequency[None, :]
    cosine = jnp.cos(angles)[:, None, :]
    sines = jnp.sin(angles)[:, None, :]
    by_head = row_data.reshape(row_data.shape[0], head_count, head_dim)
    front_half = by_head[:, :, :half_dim]
    back_half = by_head[:, :, half_dim:]
    turned = jnp.concatenate(
        [front_half * cosine - back_half * sines, back_half * cosine + front_half * sines], axis=2
    )
    return turned.reshape(row_data.shape)


def local(
    hidden,
    key_cache,
    value_cache,
    page_table,
    cache_len,
    order,
    route_ids,
    w_qkv,
    w_out,
    w_router,
    w_gate_up,
    w_down,
):
    step_count = hidden.shape[0]
    requests = hidden.shape[1]
    width_loc = hidden.shape[2]
    pages_loc = key_cache.shape[0]
    page_size = key_cache.shape[1]
    cols_loc = key_cache.shape[2]
    heads_loc = cols_loc // HEAD_DIM
    width_all = width_loc * lax.axis_size("seq")
    experts_loc = w_gate_up.shape[0]
    ff_loc = w_gate_up.shape[3]
    expert_count = w_router.shape[1]
    expert_base = lax.axis_index("col") * experts_loc
    seq_index = lax.axis_index("seq")
    score_scale = HEAD_DIM ** (-0.5)
    placing = (order[:, None] == jnp.arange(requests)[None, :]).astype(jnp.bfloat16)
    needed = (cache_len + step_count + page_size - 1) // page_size
    columns = jnp.arange(page_table.shape[1])
    in_use = columns[None, :] < needed[:, None]
    local_pages = page_table - seq_index * pages_loc
    page_hits = in_use[:, :, None] & (
        local_pages[:, :, None] == jnp.arange(pages_loc)[None, None, :]
    )
    owned_by = jnp.any(page_hits, axis=1)
    page_starts = jnp.sum(jnp.where(page_hits, columns[None, :, None] * page_size, 0), axis=(0, 1))
    page_len = jnp.sum(jnp.where(owned_by, cache_len[:, None], 0), axis=0)
    is_valid = page_starts[:, None] + jnp.arange(page_size)[None, :] < page_len[:, None]
    owner_pages = owned_by.T
    owner_float = owner_pages.astype(jnp.float32)
    owner_half = owner_pages.astype(jnp.bfloat16)
    keys_local = key_cache.reshape(pages_loc, page_size, heads_loc, HEAD_DIM)
    values_local = value_cache.reshape(pages_loc, page_size, heads_loc, HEAD_DIM)
    w_proj = w_qkv.reshape(width_loc, 3 * cols_loc)
    w_pair = w_gate_up.reshape(experts_loc, width_all, 2 * ff_loc)
    expert_ids = jnp.arange(expert_count)
    known_keys = jnp.zeros((step_count, requests, cols_loc), jnp.bfloat16)
    known_values = jnp.zeros((step_count, requests, cols_loc), jnp.bfloat16)
    attend_known_keys = known_keys
    attend_known_values = known_values
    row_count = step_count * requests
    inputs = jnp.einsum("nsc,sr->nrc", hidden, placing, preferred_element_type=jnp.float32).astype(
        jnp.bfloat16
    )
    wide_in = inputs.astype(jnp.float32)
    squares = jnp.sum(wide_in * wide_in, axis=2)
    partial_value = jnp.dot(
        inputs.reshape(row_count, width_loc), w_proj, preferred_element_type=jnp.float32
    )
    squares, partial_value = lax.psum((squares, partial_value), "seq")
    inv_one = lax.rsqrt(squares.reshape(row_count) / width_all + EPSILON)
    partial_value = partial_value * inv_one[:, None]
    positions = (cache_len[None, :] + 0 + jnp.arange(step_count)[:, None]).reshape(row_count)
    query = rotate(partial_value[:, :cols_loc], positions, HEAD_DIM).astype(jnp.bfloat16)
    fresh_key = rotate(partial_value[:, cols_loc : 2 * cols_loc], positions, HEAD_DIM).astype(
        jnp.bfloat16
    )
    fresh_value = partial_value[:, 2 * cols_loc :].astype(jnp.bfloat16)
    attend_known_keys = attend_known_keys.at[0 : 0 + step_count].set(
        fresh_key.reshape(step_count, requests, cols_loc)
    )
    attend_known_values = attend_known_values.at[0 : 0 + step_count].set(
        fresh_value.reshape(step_count, requests, cols_loc)
    )
    query_heads = query.reshape(step_count, requests, heads_loc, HEAD_DIM)
    page_query = jnp.einsum(
        "pr,nrhd->nphd", owner_half, query_heads, preferred_element_type=jnp.float32
    ).astype(jnp.bfloat16)
    scores = (
        jnp.einsum("pthd,nphd->npth", keys_local, page_query, preferred_element_type=jnp.float32)
        * score_scale
    )
    in_page = is_valid[None, :, :, None]
    scores = jnp.where(in_page, scores, LOWEST)
    page_peak = jnp.max(scores, axis=2)
    owner_mask = owner_pages[None, :, :, None]
    req_peak = jnp.max(jnp.where(owner_mask, page_peak[:, :, None, :], LOWEST), axis=1)
    back_peak = jnp.max(jnp.where(owner_mask, req_peak[:, None, :, :], LOWEST), axis=2)
    weights = jnp.where(in_page, jnp.exp(scores - back_peak[:, :, None, :]), 0.0)
    page_total = jnp.sum(weights, axis=2)
    page_sums = jnp.einsum(
        "npth,pthd->nphd",
        weights.astype(jnp.bfloat16),
        values_local,
        preferred_element_type=jnp.float32,
    )
    weight_sum = jnp.einsum("pr,nph->nrh", owner_float, page_total, precision=lax.Precision.HIGHEST)
    value_sum = jnp.einsum(
        "pr,nphd->nrhd", owner_float, page_sums, precision=lax.Precision.HIGHEST
    ).reshape(step_count, requests, cols_loc)
    top_score = lax.pmax(req_peak, "seq")
    rescale = jnp.exp(req_peak - top_score)
    scaled_values = (
        value_sum.reshape(step_count, requests, heads_loc, HEAD_DIM) * rescale[..., None]
    ).reshape(step_count, requests, cols_loc)
    weight_sum, value_sum = lax.psum((weight_sum * rescale, scaled_values), "seq")
    known_heads = attend_known_keys.reshape(step_count, requests, heads_loc, HEAD_DIM)
    fresh_scores = (
        jnp.einsum("nrhd,urhd->nruh", query_heads, known_heads, preferred_element_type=jnp.float32)
        * score_scale
    )
    visible = jnp.arange(step_count)[None, :] <= 0 + jnp.arange(step_count)[:, None]
    seen = visible[:, None, :, None]
    fresh_scores = jnp.where(seen, fresh_scores, LOWEST)
    best_score = jnp.maximum(top_score, jnp.max(fresh_scores, axis=2))
    fresh_weights = jnp.where(seen, jnp.exp(fresh_scores - best_score[:, :, None, :]), 0.0)
    cache_factor = jnp.exp(top_score - best_score)
    denominator = weight_sum * cache_factor + jnp.sum(fresh_weights, axis=2)
    fresh_sums = jnp.einsum(
        "nruh,urhd->nrhd",
        fresh_weights.astype(jnp.bfloat16),
        attend_known_values.reshape(step_count, requests, heads_loc, HEAD_DIM),
        preferred_element_type=jnp.float32,
    )
    numerator = (
        value_sum.reshape(step_count, requests, heads_loc, HEAD_DIM) * cache_factor[..., None]
        + fresh_sums
    )
    attended = (
        (numerator / denominator[..., None]).reshape(row_count, cols_loc).astype(jnp.bfloat16)
    )
    projected = lax.psum(jnp.dot(attended, w_out, preferred_element_type=jnp.float32), "col")
    residual = (wide_in.reshape(row_count, width_loc) + projected).astype(jnp.bfloat16)
    chosen = route_ids.reshape(row_count, 2)
    mid_steps = residual.reshape(step_count, requests, width_loc)
    shard_rows = lax.all_gather(mid_steps, "seq", axis=2, tiled=True)
    flat_rows = shard_rows.reshape(row_count, shard_rows.shape[2])
    pair_sum = jnp.einsum("rc,ecf->ref", flat_rows, w_pair, preferred_element_type=jnp.float32)
    wide_rows = flat_rows.astype(jnp.float32)
    square_sum = jnp.sum(wide_rows * wide_rows, axis=1)
    router_sum = jnp.dot(flat_rows, w_router, preferred_element_type=jnp.float32)
    pair_sum, square_sum, router_sum = (pair_sum, square_sum, router_sum)
    inv_two = lax.rsqrt(square_sum / width_all + EPSILON)
    logits = router_sum * inv_two[:, None]
    first_pick = chosen[:, 0:1] == expert_ids[None, :]
    second_pick = chosen[:, 1:2] == expert_ids[None, :]
    first_share = jax.nn.sigmoid(
        jnp.sum(jnp.where(first_pick, logits, 0.0), axis=1)
        - jnp.sum(jnp.where(second_pick, logits, 0.0), axis=1)
    )
    gate_rows = jnp.where(first_pick, first_share[:, None], 0.0) + jnp.where(
        second_pick, 1.0 - first_share[:, None], 0.0
    )
    gate_local = lax.dynamic_slice_in_dim(gate_rows, expert_base, experts_loc, 1)
    pair_sum = pair_sum * inv_two[:, None, None]
    active = (jax.nn.silu(pair_sum[..., :ff_loc]) * pair_sum[..., ff_loc:]).astype(jnp.bfloat16)
    outputs = jnp.einsum("ref,efd->red", active, w_down, preferred_element_type=jnp.float32)
    weighted = jnp.sum(outputs * gate_local[:, :, None], axis=1)
    spread = lax.psum_scatter(weighted, "seq", scatter_dimension=1, tiled=True)
    mixture = lax.psum(spread, "col")
    layer_rows = (
        (residual.astype(jnp.float32) + mixture)
        .astype(jnp.bfloat16)
        .reshape(step_count, requests, width_loc)
    )
    return (layer_rows, attend_known_keys, attend_known_values)


def solution(mesh):
    placed = (
        P(None, None, "seq"),
        P("seq", None, "col"),
        P("seq", None, "col"),
        P(),
        P(),
        P(),
        P(),
        P("seq", None, "col"),
        P("col", "seq"),
        P(),
        P("col", None, None, "seq"),
        P("col", "seq", None),
    )
    return jax.shard_map(
        local,
        mesh=mesh,
        in_specs=placed,
        out_specs=(P(None, None, "seq"), P(None, None, "col"), P(None, None, "col")),
        check_vma=False,
    )
```

profile of v0, /device:TPU:0, one launch (start us, length us, event | category | flops | bytes accessed | tf_op | source)
XLA Modules:
  0.0 747.3 jit_solution(15203284363969013890)
XLA Ops:
  7.2 1.2 fusion.25
  9.4 1.2 copy.147
  10.6 3.0 fusion.35
  14.5 1.7 fusion.2
  16.3 45.6 %psum.43 = f32[4,96]{1,0:T(4,128)S(1)} all-reduce(f32[4,96]{1,0:T(4,128)S(1)} %get-tuple-element.66), channel_id=1, replica_groups=mesh['seq'=16,'col'=2] {'seq'}, use_global_device_ids=true, to_apply=%region_5.6 | all-reduce | flops 384 | bytes 3072 | tf_op jit(solution)/shard_map/psum | solution.py:92
  62.1 24.6 %copy.109 = bf16[72,128,1024]{1,2,0:T(8,128)(2,1)} copy(bf16[72,128,1024]{2,1,0:T(8,128)(2,1)} %param.21) | data formatting | bytes 37748736 | tf_op args[1]
  86.7 24.7 %copy.114 = bf16[72,128,1024]{1,2,0:T(8,128)(2,1)} copy(bf16[72,128,1024]{2,1,0:T(8,128)(2,1)} %param.22) | data formatting | bytes 37748736 | tf_op args[2]
  111.5 1.1 select_reduce_fusion
  113.6 83.1 %all-reduce.5.cloned.1.call-done = f32[384,3072]{1,0:T(8,128)} async-done(((f32[384,3072]{1,0:T(8,128)}), f32[384,3072]{1,0:T(8,128)}) %all-reduce.5.cloned.1.call-update) | async-done | bytes 4718608 | tf_op jit(solution)/shard_map/psum | solution.py:92
  196.7 2.8 broadcast_multiply_fusion
  199.5 1.6 fusion.34
  204.8 2.6 copy.119
  207.4 2.2 copy.110
  209.6 9.4 %bitcast_reduce_fusion = (f32[4,72,16]{0,2,1:T(8,128)S(1)}, f32[72,16,4,128]{3,2,1,0:T(4,128)S(1)}) fusion(pred[72,128]{1,0:T(8,128)(4,1)S(1)} %add_compare_fusion, bf16[4,72,16,64]{3,0,2,1:T(4,128)(2,1)} %copy.110, bf16[72,128,16,64]{1,3,2,0:T(8,128)(2,1)} %bitcast.105), kind=kOutput, calls=%fused_computation.8 | convolution fusion | flops 77262336 | bytes 21851136 | tf_op jit(solution)/shard_map/pthd,nphd->npth/dot_general | solution.py:112
  220.4 75.6 %pmax.7 = f32[4,96,16]{1,2,0:T(8,128)} all-reduce(f32[4,96,16]{1,2,0:T(8,128)S(1)} %select_reduce_fusion.2), channel_id=1, replica_groups=mesh['seq'=16,'col'=2] {'seq'}, use_global_device_ids=true, to_apply=%region_9.10 | all-reduce | flops 6144 | bytes 49152 | tf_op jit(solution)/shard_map/pmax | solution.py:133
  296.0 1.4 select_reduce_fusion.1
  297.3 3.0 copy.117
  300.4 1.6 multiply_subtract_fusion
  302.1 1.6 convert_element_type.87
  303.7 4.3 copy.118
  308.0 5.3 fusion.36
  313.3 3.7 copy.120
  317.0 1.4 copy.113
  318.4 1.1 fusion.22
  320.2 14.0 %convolution_bitcast_fusion = f32[4,72,16,64]{3,0,2,1:T(4,128)S(1)} fusion(bf16[72,128,16,64]{1,3,2,0:T(8,128)(2,1)} %bitcast.106, f32[72,16,4,128]{3,2,1,0:T(4,128)S(1)} %get-tuple-element.81, f32[4,72,16]{0,2,1:T(8,128)S(1)} %copy.113, pred[72,128]{1,0:T(8,128)(4,1)} %copy-done.12), kind=kOutput, calls=%fused_computation.24 | convolution fusion | flops 78446592 | bytes 22440960 | tf_op jit(solution)/shard_map/npth,pthd->nphd/dot_general | solution.py:123
  334.2 4.2 bitcast_multiply_fusion.1
  338.5 1.6 slice.111
  340.0 1.9 reshape.362
  342.0 5.0 fusion.20
  346.9 1.9 copy.127
  348.9 1.6 fusion.23
  350.5 3.2 copy.125
  353.7 3.7 fusion.12
  357.3 3.1 copy.126
  361.4 72.0 %psum.45 = f32[4,96,16]{1,2,0:T(8,128)S(1)} all-reduce(f32[4,96,16]{1,2,0:T(8,128)S(1)} %fusion.16), channel_id=1, replica_groups=mesh['seq'=16,'col'=2] {'seq'}, use_global_device_ids=true, to_apply=%region_13.14 | all-reduce | flops 6144 | bytes 49152 | tf_op jit(solution)/shard_map/psum | solution.py:138
  434.2 26.6 %all-reduce.7.cloned.1.call-done = f32[4,96,16,64]{1,3,2,0:T(8,128)} async-done(((f32[4,96,16,64]{1,3,2,0:T(8,128)}), f32[4,96,16,64]{1,3,2,0:T(8,128)}) %all-reduce.7.cloned.1.call-update) | async-done | bytes 1572880 | tf_op jit(solution)/shard_map/psum | solution.py:138
  460.8 2.8 fusion.9
  466.6 17.4 %all-reduce.9.cloned.1.call-done = f32[384,144]{0,1:T(8,128)} async-done(((f32[384,144]{0,1:T(8,128)}), f32[384,144]{0,1:T(8,128)}) %all-reduce.9.cloned.1.call-update) | async-done | bytes 221200 | tf_op jit(solution)/shard_map/psum | solution.py:164
  485.9 64.8 %all-gather.2.cloned.1.call-done = bf16[4,96,2304]{1,0,2:T(4,128)(2,1)} async-done(((bf16[4,96,144]{1,0,2:T(4,128)(2,1)}), bf16[4,96,2304]{1,0,2:T(4,128)(2,1)}) %all-gather.2.cloned.1.call-update) | async-done | bytes 1769488 | tf_op jit(solution)/shard_map/all_gather | solution.py:168
  550.7 4.2 multiply_reduce_fusion
  555.0 3.8 copy.132
  558.8 2.1 select_reduce_fusion.4
  560.9 10.3 %broadcast_multiply_fusion.1 = f32[384,4,720]{0,2,1:T(8,128)S(1)} fusion(f32[384]{0:T(512)S(1)} %rsqrt.27, bf16[384,2304,1]{1,0,2:T(8,128)(2,1)} %bitcast.108, bf16[4,2304,720]{1,2,0:T(8,128)(2,1)} %bitcast.117), kind=kOutput, calls=%fused_computation.19 | convolution fusion | flops 5097185280 | bytes 19465728 | tf_op jit(solution)/shard_map/rc,ecf->ref/dot_general | solution.py:170
  571.3 9.8 %fusion = f32[384,2304]{1,0:T(8,128)} fusion(bf16[4,360,2304]{2,1,0:T(8,128)(2,1)} %param.31, f32[384,4]{0,1:T(4,128)S(1)} %select_add_fusion, f32[384,4,720]{0,2,1:T(8,128)S(1)} %broadcast_multiply_fusion.1), kind=kOutput, calls=%fused_computation.1 | convolution fusion | flops 2557550592 | bytes 14604288 | tf_op jit(solution)/shard_map/ref,efd->red/dot_general | solution.py:189
  581.0 5.2 copy.134
  586.2 132.4 %reduce-scatter.2.cloned.1.call-done = f32[384,144]{0,1:T(8,128)} async-done(((f32[384,2304]{0,1:T(8,128)}), f32[384,144]{0,1:T(8,128)}) %reduce-scatter.2.cloned.1.call-update) | async-done | bytes 221200 | tf_op jit(solution)/shard_map/reduce_scatter | solution.py:191
  719.3 1.4 copy.136
  720.7 17.5 %all-reduce.11.cloned.1.call-done = f32[384,144]{0,1:T(8,128)} async-done(((f32[384,144]{0,1:T(8,128)}), f32[384,144]{0,1:T(8,128)}) %all-reduce.11.cloned.1.call-update) | async-done | bytes 221200 | tf_op jit(solution)/shard_map/psum | solution.py:192
  (93 shorter events, 17.9 us)
Async XLA Ops:
  7.2 458.1 %copy-start = (bf16[1024,144]{0,1:T(8,128)(2,1)S(1)}, bf16[1024,144]{0,1:T(8,128)(2,1)}, u32[]{:S(2)}) copy-start(bf16[1024,144]{0,1:T(8,128)(2,1)} %param.28) | copy-start | bytes 884740
  7.2 189.5 %all-reduce.5.cloned.1.call-start = ((), (), s32[]{:S(2)}) async-start(), calls=%async_computation.1 | async-start | bytes 9437184 | tf_op jit(solution)/shard_map/psum | solution.py:92
  8.5 0.7 copy-start.7
  13.6 0.7 copy-start.16
  13.6 0.8 copy-start.13
  13.6 447.2 %all-reduce.7.cloned.1.call-start = ((), (), s32[]{:S(2)}) async-start(), calls=%async_computation.2 | async-start | bytes 4194304 | tf_op jit(solution)/shard_map/psum | solution.py:138
  112.7 96.9 %copy-start.12 = (pred[72,128]{1,0:T(8,128)(4,1)}, pred[72,128]{1,0:T(8,128)(4,1)S(1)}, u32[]{:S(2)}) copy-start(pred[72,128]{1,0:T(8,128)(4,1)S(1)} %add_compare_fusion) | copy-start | bytes 27652
  199.5 2.6 copy-start.1
  219.1 81.3 %copy-start.9 = (f32[384,32]{0,1:T(8,128)S(1)}, f32[384,32]{0,1:T(8,128)}, u32[]{:S(2)}) copy-start(f32[384,32]{0,1:T(8,128)} %get-tuple-element.79) | copy-start | bytes 147460
  302.1 11.2 %copy-start.3 = (bf16[384,16,64]{0,2,1:T(8,128)(2,1)}, bf16[384,16,64]{0,2,1:T(8,128)(2,1)S(1)}, u32[]{:S(2)}) copy-start(bf16[384,16,64]{0,2,1:T(8,128)(2,1)S(1)} %maximum_convert_fusion) | copy-start | bytes 2359300
  313.3 6.2 copy-start.10
  318.4 15.8 %copy-start.6 = (f32[4,72,16]{0,2,1:T(8,128)}, f32[4,72,16]{0,2,1:T(8,128)S(1)}, u32[]{:S(2)}) copy-start(f32[4,72,16]{0,2,1:T(8,128)S(1)} %copy.113) | copy-start | bytes 55300
  338.4 145.5 %all-reduce.9.cloned.1.call-start = ((), (), s32[]{:S(2)}) async-start(), calls=%async_computation.3 | async-start | bytes 442368 | tf_op jit(solution)/shard_map/psum | solution.py:164
  340.0 6.9 copy-start.5
  342.0 6.9 copy-start.11
  463.6 2.7 copy-start.8
  464.6 21.2 %copy-start.15 = (s32[4,96,2]{1,2,0:T(2,128)S(1)}, s32[4,96,2]{1,2,0:T(2,128)}, u32[]{:S(2)}) copy-start(s32[4,96,2]{1,2,0:T(2,128)} %param.26) | copy-start | bytes 9220
  466.3 84.4 %all-gather.2.cloned.1.call-start = ((), (), s32[]{:S(2)}) async-start(), calls=%async_computation.4 | async-start | bytes 2506752 | tf_op jit(solution)/shard_map/all_gather | solution.py:168
  485.7 232.9 %reduce-scatter.2.cloned.1.call-start = ((), (), s32[]{:S(2)}) async-start(), calls=%async_computation.5 | async-start | bytes 3760128 | tf_op jit(solution)/shard_map/reduce_scatter | solution.py:191
  550.7 4.4 copy-start.2
  554.9 3.9 copy-start.14
  586.2 132.5 %copy-start.4 = (bf16[384,16,64]{0,2,1:T(8,128)(2,1)S(1)}, bf16[384,16,64]{0,2,1:T(8,128)(2,1)}, u32[]{:S(2)}) copy-start(bf16[384,16,64]{0,2,1:T(8,128)(2,1)} %copy-done.3) | copy-start | bytes 2359300
  586.2 152.0 %all-reduce.11.cloned.1.call-start = ((), (), s32[]{:S(2)}) async-start(), calls=%async_computation.6 | async-start | bytes 442368 | tf_op jit(solution)/shard_map/psum | solution.py:192
Sparse Core Ops, SparseCore 0:
  13.8 182.9 all-reduce.4
  338.5 122.2 all-reduce.6
  466.4 17.4 all-reduce.8
  487.2 63.4 all-gather.1
  586.3 132.2 reduce-scatter.1
  720.8 17.3 all-reduce.10
where the time goes:
time: 757 us; the launch traced here: 747 us
  waiting for transfers between devices  342 us (45%)
  blocking collectives  193 us (25%)
  local copies, waits for them, and re-layouts  102 us (13%)
  matrix products  65.4 us (9%)
  other arithmetic  30 us (4%)
  between operations  15 us (2%)
    reduce_scatter x1, waiting for transfers between devices, local(): spread = lax.psum_scatter(weighted, 'seq', scatter_dimension=1, tiled=True)  132 us
    psum x1, waiting for transfers between devices, local(): squares, partial_value = lax.psum((squares, partial_value), 'seq')  83.1 us
    pmax x1, blocking collectives, local(): top_score = lax.pmax(req_peak, 'seq')  75.6 us
    psum x1, blocking collectives, local(): lax.psum((weight_sum * rescale, scaled_values), 'seq')  72 us
    all_gather x1, waiting for transfers between devices, local(): shard_rows = lax.all_gather(mid_steps, 'seq', axis=2, tiled=True)  64.8 us
    unnamed x39, local copies, waits for them, and re-layouts  53.7 us
    psum x1, blocking collectives, local(): squares, partial_value = lax.psum((squares, partial_value), 'seq')  45.6 us
    psum x1, waiting for transfers between devices, local(): lax.psum((weight_sum * rescale, scaled_values), 'seq')  26.6 us
  transfers between devices with their start and end apart: 6, of which 6 were waited for; matrix products, arithmetic and copies ran while one was open for 11% of the time, Pallas kernels for 0%

commit v1 on v0

v1 whole, which is shorter than its diff:
```python
import jax
import jax.numpy as jnp
from jax import lax
from jax.experimental import pallas as pl
from jax.experimental.pallas import tpu as pltpu
from jax.sharding import PartitionSpec as P

HEAD_DIM = 64


EPSILON = 1e-05
LOWEST = -1e30


def rotate(row_data, positions, head_dim):
    head_count = row_data.shape[1] // head_dim
    half_dim = head_dim // 2
    frequency = jnp.exp(
        -jnp.log(10000.0) * 2.0 * jnp.arange(half_dim, dtype=jnp.float32) / head_dim
    )
    angles = positions.astype(jnp.float32)[:, None] * frequency[None, :]
    cosine = jnp.cos(angles)[:, None, :]
    sines = jnp.sin(angles)[:, None, :]
    by_head = row_data.reshape(row_data.shape[0], head_count, head_dim)
    front_half = by_head[:, :, :half_dim]
    back_half = by_head[:, :, half_dim:]
    turned = jnp.concatenate(
        [front_half * cosine - back_half * sines, back_half * cosine + front_half * sines], axis=2
    )
    return turned.reshape(row_data.shape)


def attend_kernel(owner_ref, count_ref, q_ref, k_ref, v_ref, sum_ref, peak_ref, total_ref):
    page = pl.program_id(0)
    steps, cols = q_ref.shape[1], q_ref.shape[2]
    size = k_ref.shape[1]
    padded = peak_ref.shape[2] // steps
    count = count_ref[page]
    wide = q_ref[0].astype(jnp.float32)
    own = lax.broadcasted_iota(jnp.int32, (padded, cols), 1) // HEAD_DIM == lax.broadcasted_iota(
        jnp.int32, (padded, cols), 0
    )
    spread = jnp.concatenate(
        [jnp.where(own, wide[n : n + 1, :], 0.0) for n in range(steps)], axis=0
    ).astype(jnp.bfloat16)
    scores = lax.dot_general(
        k_ref[0], spread, (((1,), (1,)), ((), ())), preferred_element_type=jnp.float32
    ) * (HEAD_DIM ** (-0.5))
    live = lax.broadcasted_iota(jnp.int32, (size, steps * padded), 0) < count
    scores = jnp.where(live, scores, LOWEST)
    peak = jnp.max(scores, axis=0, keepdims=True)
    weights = jnp.where(live, jnp.exp(scores - peak), 0.0)
    peak_ref[0] = peak
    total_ref[0] = jnp.sum(weights, axis=0, keepdims=True)
    mixed = lax.dot_general(
        weights.astype(jnp.bfloat16),
        v_ref[0],
        (((0,), (0,)), ((), ())),
        preferred_element_type=jnp.float32,
    )
    for n in range(steps):
        part = jnp.where(own, mixed[n * padded : (n + 1) * padded, :], 0.0)
        sum_ref[0, n : n + 1, :] = jnp.sum(part, axis=0, keepdims=True)


def attend_pages(owner, count, query, keys, values):
    pages, size, cols = keys.shape
    steps = query.shape[1]
    heads = cols // HEAD_DIM
    padded = -(-heads // 8) * 8
    sums, peak, total = pl.pallas_call(
        attend_kernel,
        grid_spec=pltpu.PrefetchScalarGridSpec(
            num_scalar_prefetch=2,
            grid=(pages,),
            in_specs=[
                pl.BlockSpec((1, steps, cols), lambda p, o, c: (o[p], 0, 0)),
                pl.BlockSpec((1, size, cols), lambda p, o, c: (p, 0, 0)),
                pl.BlockSpec((1, size, cols), lambda p, o, c: (p, 0, 0)),
            ],
            out_specs=[
                pl.BlockSpec((1, steps, cols), lambda p, o, c: (p, 0, 0)),
                pl.BlockSpec((1, 1, steps * padded), lambda p, o, c: (p, 0, 0)),
                pl.BlockSpec((1, 1, steps * padded), lambda p, o, c: (p, 0, 0)),
            ],
        ),
        out_shape=(
            jax.ShapeDtypeStruct((pages, steps, cols), jnp.float32),
            jax.ShapeDtypeStruct((pages, 1, steps * padded), jnp.float32),
            jax.ShapeDtypeStruct((pages, 1, steps * padded), jnp.float32),
        ),
        cost_estimate=pl.CostEstimate(
            flops=4 * pages * steps * padded * size * cols,
            bytes_accessed=4 * pages * size * cols,
            transcendentals=pages * steps * padded * size,
        ),
    )(owner, count, query, keys, values)
    peak = peak.reshape(pages, steps, padded)[:, :, :heads]
    total = total.reshape(pages, steps, padded)[:, :, :heads]
    return sums, peak, total


def pieces(value, count):
    out = []
    for _ in range(count):
        part = lax.reduce_precision(value, 8, 7)
        out.append(part.astype(jnp.bfloat16))
        value = value - part
    return out


def exchange(blocks):
    return lax.all_to_all(blocks, "seq", split_axis=0, concat_axis=0, tiled=True)


def col_scatter(rows):
    if lax.axis_size("col") == 2:
        half = rows.shape[0] // 2
        me = lax.axis_index("col")
        mine = lax.dynamic_slice_in_dim(rows, me * half, half, 0)
        theirs = lax.dynamic_slice_in_dim(rows, (1 - me) * half, half, 0)
        return mine + lax.ppermute(theirs, "col", [(0, 1), (1, 0)])
    return lax.psum_scatter(rows, "col", scatter_dimension=0, tiled=True)


def col_gather(rows):
    if lax.axis_size("col") == 2:
        me = lax.axis_index("col")
        other = lax.ppermute(rows, "col", [(0, 1), (1, 0)])
        first = jnp.where(me == 0, rows, other)
        second = jnp.where(me == 0, other, rows)
        return jnp.concatenate([first, second], axis=0)
    return lax.all_gather(rows, "col", axis=0, tiled=True)


def local(
    hidden,
    key_cache,
    value_cache,
    page_table,
    cache_len,
    order,
    route_ids,
    w_qkv,
    w_out,
    w_router,
    w_gate_up,
    w_down,
):
    steps, requests, width_loc = hidden.shape
    pages_loc, page_size, cols = key_cache.shape
    heads = cols // HEAD_DIM
    shards = lax.axis_size("seq")
    width_all = width_loc * shards
    experts_loc = w_gate_up.shape[0]
    ff_loc = w_gate_up.shape[3]
    expert_count = w_router.shape[1]
    expert_base = lax.axis_index("col") * experts_loc
    seq_index = lax.axis_index("seq")
    share = -(-requests // shards)
    filler = share * shards - requests
    row_count = steps * requests
    own_rows = share * steps

    placing = (order[:, None] == jnp.arange(requests)[None, :]).astype(jnp.bfloat16)
    inputs = jnp.einsum("nsc,sr->rnc", hidden, placing, preferred_element_type=jnp.float32).astype(
        jnp.bfloat16
    )
    flat_in = inputs.reshape(row_count, width_loc)
    wide_in = flat_in.astype(jnp.float32)
    squares = jnp.sum(wide_in * wide_in, axis=1, keepdims=True)
    partial = jnp.dot(
        flat_in, w_qkv.reshape(width_loc, 3 * cols), preferred_element_type=jnp.float32
    ).astype(jnp.bfloat16)
    tail = jnp.pad(jnp.concatenate(pieces(squares, 3), axis=1), ((0, 0), (0, 125)))
    sent = jnp.pad(jnp.concatenate([partial, tail], axis=1), ((0, filler * steps), (0, 0)))
    sent = sent.reshape(shards, own_rows, 3 * cols + 128)
    got = jnp.sum(exchange(sent).astype(jnp.float32), axis=0)
    inv_one = lax.rsqrt(jnp.sum(got[:, 3 * cols :], axis=1) / width_all + EPSILON)
    proj = got[:, : 3 * cols] * inv_one[:, None]
    own_len = lax.dynamic_slice_in_dim(jnp.pad(cache_len, (0, filler)), seq_index * share, share, 0)
    positions = (own_len[:, None] + jnp.arange(steps)[None, :]).reshape(own_rows)
    query = rotate(proj[:, :cols], positions, HEAD_DIM).astype(jnp.bfloat16)
    fresh_key = rotate(proj[:, cols : 2 * cols], positions, HEAD_DIM).astype(jnp.bfloat16)
    fresh_value = proj[:, 2 * cols :].astype(jnp.bfloat16)
    all_query = lax.all_gather(query, "seq", axis=0, tiled=True)[:row_count]
    all_query, fresh_pair = lax.optimization_barrier(
        (all_query, jnp.concatenate([fresh_key, fresh_value], axis=1))
    )
    all_pair = lax.all_gather(fresh_pair, "seq", axis=0, tiled=True)[:row_count]
    all_pair = all_pair.reshape(requests, steps, 2 * cols).transpose(1, 0, 2)

    needed = (cache_len + steps + page_size - 1) // page_size
    columns = jnp.arange(page_table.shape[1])
    in_use = columns[None, :] < needed[:, None]
    local_pages = page_table - seq_index * pages_loc
    page_hits = in_use[:, :, None] & (
        local_pages[:, :, None] == jnp.arange(pages_loc)[None, None, :]
    )
    owned_by = jnp.any(page_hits, axis=1)
    page_starts = jnp.sum(jnp.where(page_hits, columns[None, :, None] * page_size, 0), axis=(0, 1))
    page_len = jnp.sum(jnp.where(owned_by, cache_len[:, None], 0), axis=0)
    owner = jnp.sum(jnp.where(owned_by, jnp.arange(requests)[:, None], 0), axis=0)
    count = page_len - page_starts
    page_sums, page_peak, page_total = attend_pages(
        owner.astype(jnp.int32),
        count.astype(jnp.int32),
        all_query.reshape(requests, steps, cols),
        key_cache,
        value_cache,
    )
    mask = owned_by[:, :, None, None]
    req_peak = jnp.max(jnp.where(mask, page_peak[None], LOWEST), axis=1)
    back_peak = jnp.max(jnp.where(mask, req_peak[:, None], LOWEST), axis=0)
    factor = jnp.exp(page_peak - back_peak)
    factor = jnp.where((count > 0)[:, None, None] & jnp.any(owned_by, axis=0)[:, None, None], factor, 0.0)
    owner_float = owned_by.astype(jnp.float32)
    req_total = jnp.einsum(
        "rp,pnh->rnh", owner_float, page_total * factor, precision=lax.Precision.HIGHEST
    )
    scaled = page_sums * jnp.repeat(factor, HEAD_DIM, axis=2)
    req_sums = jnp.einsum("rp,pnc->rnc", owner_float, scaled, precision=lax.Precision.HIGHEST)
    extra = jnp.concatenate(pieces(req_peak, 3) + pieces(req_total, 3), axis=2)
    spare = -extra.shape[2] % 128
    extra = jnp.pad(extra, ((0, 0), (0, 0), (0, spare)))
    sent = jnp.concatenate([req_sums.astype(jnp.bfloat16), extra], axis=2)
    sent = jnp.pad(sent, ((0, filler), (0, 0), (0, 0)))
    got = exchange(sent.reshape(shards, own_rows, sent.shape[2])).astype(jnp.float32)
    sums = got[:, :, :cols]
    bits = got[:, :, cols : cols + 6 * heads].reshape(shards, own_rows, 6, heads)
    peaks = bits[:, :, 0] + bits[:, :, 1] + bits[:, :, 2]
    totals = bits[:, :, 3] + bits[:, :, 4] + bits[:, :, 5]
    q_own = query.astype(jnp.float32).reshape(share, steps, 1, heads, HEAD_DIM)
    k_own = fresh_key.astype(jnp.float32).reshape(share, 1, steps, heads, HEAD_DIM)
    v_own = fresh_value.astype(jnp.float32).reshape(share, 1, steps, cols)
    fresh_scores = jnp.sum(q_own * k_own, axis=4) * (HEAD_DIM ** (-0.5))
    seen = (jnp.arange(steps)[None, :] <= jnp.arange(steps)[:, None])[None, :, :, None]
    fresh_scores = jnp.where(seen, fresh_scores, LOWEST)
    best = jnp.maximum(
        jnp.max(peaks, axis=0).reshape(share, steps, heads), jnp.max(fresh_scores, axis=2)
    )
    fresh_weights = jnp.where(seen, jnp.exp(fresh_scores - best[:, :, None]), 0.0)
    scale = jnp.exp(peaks - best.reshape(1, own_rows, heads))
    denominator = jnp.sum(totals * scale, axis=0) + jnp.sum(fresh_weights, axis=2).reshape(
        own_rows, heads
    )
    lowered = lax.reduce_precision(fresh_weights, 8, 7)
    numerator = jnp.sum(sums * jnp.repeat(scale, HEAD_DIM, axis=2), axis=0) + jnp.sum(
        jnp.repeat(lowered, HEAD_DIM, axis=3) * v_own, axis=2
    ).reshape(own_rows, cols)
    attended = (numerator / jnp.repeat(denominator, HEAD_DIM, axis=1)).astype(jnp.bfloat16)
    all_attended = lax.all_gather(attended, "seq", axis=0, tiled=True)[:row_count]
    projected = col_scatter(jnp.dot(all_attended, w_out, preferred_element_type=jnp.float32))
    half = projected.shape[0]
    wide_half = lax.dynamic_slice_in_dim(wide_in, lax.axis_index("col") * half, half, 0)
    residual = (wide_half + projected).astype(jnp.bfloat16)
    flat_rows = col_gather(lax.all_gather(residual, "seq", axis=1, tiled=True))

    chosen = route_ids.transpose(1, 0, 2).reshape(row_count, 2)
    expert_ids = jnp.arange(expert_count)
    w_pair = w_gate_up.reshape(experts_loc, width_all, 2 * ff_loc)
    pair_sum = jnp.einsum("rc,ecf->ref", flat_rows, w_pair, preferred_element_type=jnp.float32)
    wide_rows = flat_rows.astype(jnp.float32)
    square_sum = jnp.sum(wide_rows * wide_rows, axis=1)
    router_sum = jnp.dot(flat_rows, w_router, preferred_element_type=jnp.float32)
    inv_two = lax.rsqrt(square_sum / width_all + EPSILON)
    logits = router_sum * inv_two[:, None]
    first_pick = chosen[:, 0:1] == expert_ids[None, :]
    second_pick = chosen[:, 1:2] == expert_ids[None, :]
    first_share = jax.nn.sigmoid(
        jnp.sum(jnp.where(first_pick, logits, 0.0), axis=1)
        - jnp.sum(jnp.where(second_pick, logits, 0.0), axis=1)
    )
    gate_rows = jnp.where(first_pick, first_share[:, None], 0.0) + jnp.where(
        second_pick, 1.0 - first_share[:, None], 0.0
    )
    gate_local = lax.dynamic_slice_in_dim(gate_rows, expert_base, experts_loc, 1)
    pair_sum = pair_sum * inv_two[:, None, None]
    active = (jax.nn.silu(pair_sum[..., :ff_loc]) * pair_sum[..., ff_loc:]).astype(jnp.bfloat16)
    outputs = jnp.einsum("ref,efd->red", active, w_down, preferred_element_type=jnp.float32)
    weighted = jnp.sum(outputs * gate_local[:, :, None], axis=1)
    joined = col_scatter(weighted).astype(jnp.bfloat16)
    blocks = joined.reshape(half, shards, width_loc).transpose(1, 0, 2)
    mixture = jnp.sum(exchange(blocks).astype(jnp.float32), axis=0)
    layer_half = (residual.astype(jnp.float32) + mixture).astype(jnp.bfloat16)
    layer_rows = col_gather(layer_half).reshape(requests, steps, width_loc).transpose(1, 0, 2)
    return (layer_rows, all_pair[:, :, :cols], all_pair[:, :, cols:])


def solution(mesh):
    placed = (
        P(None, None, "seq"),
        P("seq", None, "col"),
        P("seq", None, "col"),
        P(),
        P(),
        P(),
        P(),
        P("seq", None, "col"),
        P("col", "seq"),
        P(),
        P("col", None, None, "seq"),
        P("col", "seq", None),
    )
    return jax.shard_map(
        local,
        mesh=mesh,
        in_specs=placed,
        out_specs=(P(None, None, "seq"), P(None, None, "col"), P(None, None, "col")),
        check_vma=False,
    )
```

time: 757 us -> 420 us (0.55)
  waiting for transfers between devices: 342 us -> 120 us
  local copies, waits for them, and re-layouts: 102 us -> 27.6 us
  Pallas kernels: 0 us -> 59.6 us
  blocking collectives: 193 us -> 137 us
  matrix products: 65.4 us -> 24.4 us
  starting transfers between devices: 0.25 us -> 16.2 us
  other arithmetic: 30 us -> 19.1 us
    psum x4 -> x0, waiting for transfers between devices: 145 us -> none  [the longest x1 83.1 us: local(): squares, partial_value = lax.psum((squares, partial_value), 'seq')]
    all_gather x0 -> x3, blocking collectives: none -> 137 us  [the longest x1 50.2 us: local(): all_query = lax.all_gather(query, 'seq', axis=0, tiled=True)[:row_count]]
    reduce_scatter x1 -> x0, waiting for transfers between devices: 132 us -> none  [local(): spread = lax.psum_scatter(weighted, 'seq', scatter_dimension=1, tiled=True)]
    psum x2 -> x0, blocking collectives: 118 us -> none  [the longest x1 72 us: local(): lax.psum((weight_sum * rescale, scaled_values), 'seq')]
    pmax x1 -> x0, blocking collectives: 75.6 us -> none  [local(): top_score = lax.pmax(req_peak, 'seq')]
    pallas_call x0 -> x1, Pallas kernels: none -> 59.6 us  [attend_pages(): pl.pallas_call(attend_kernel, grid_spec=pltpu.PrefetchScalarGridSpec(num_...]
    all_to_all x0 -> x3, waiting for transfers between devices: none -> 58 us  [exchange(): lax.all_to_all(blocks, 'seq', split_axis=0, concat_axis=0, tiled=True)]
    unnamed x39 -> x33, local copies, waits for them, and re-layouts: 53.7 us -> 6.03 us
  transfers between devices with their start and end apart: 6 -> 8, of which waited for: 6 -> 6; matrix products, arithmetic and copies ran while one was open for 11% -> 3% of each run, Pallas kernels for 0% -> 0%
where the time goes in v1:
time: 420 us; the launch traced here: 418 us
  blocking collectives  137 us (33%)
  waiting for transfers between devices  120 us (29%)
  Pallas kernels  59.6 us (14%)
  local copies, waits for them, and re-layouts  27.6 us (7%)
  matrix products  24.4 us (6%)
  other arithmetic  19.1 us (5%)
  starting transfers between devices  16.2 us (4%)
  between operations  14.7 us (4%)
    pallas_call x1, Pallas kernels, attend_pages(): pl.pallas_call(attend_kernel, grid_spec=pltpu.PrefetchScalarGridSpec(num_...  59.6 us
    all_to_all x3, waiting for transfers between devices, exchange(): lax.all_to_all(blocks, 'seq', split_axis=0, concat_axis=0, tiled=True)  58 us
    all_gather x1, waiting for transfers between devices, local(): all_pair = lax.all_gather(fresh_pair, 'seq', axis=0, tiled=True)[:row_count]  54.4 us
    all_gather x1, blocking collectives, local(): all_query = lax.all_gather(query, 'seq', axis=0, tiled=True)[:row_count]  50.2 us
    all_gather x1, blocking collectives, local(): lax.all_gather(attended, 'seq', axis=0, tiled=True)[:row_count]  43.6 us
    all_gather x1, blocking collectives, local(): flat_rows = col_gather(lax.all_gather(residual, 'seq', axis=1, tiled=True))  42.7 us
    all_to_all x3, starting transfers between devices, exchange(): lax.all_to_all(blocks, 'seq', split_axis=0, concat_axis=0, tiled=True)  15.8 us
    dot_general x1, matrix products, local(): jnp.einsum('rc,ecf->ref', flat_rows, w_pair, preferred_element_type=jnp.f...  12 us
  transfers between devices with their start and end apart: 8, of which 6 were waited for; matrix products, arithmetic and copies ran while one was open for 3% of the time, Pallas kernels for 0%

profile of v1, /device:TPU:0, one launch (start us, length us, event | category | flops | bytes accessed | tf_op | source)
XLA Modules:
  0.0 417.7 jit_solution(16460617497755540050)
XLA Ops:
  7.2 1.3 fusion.20
  9.4 0.8 convolution_convert_fusion
  10.1 1.6 fusion.5
  11.8 8.4 %all-to-all-start = ((bf16[16,24,3200]{2,1,0:T(8,128)(2,1)}), bf16[16,24,3200]{2,1,0:T(8,128)(2,1)S(1)}, u32[]{:S(2)}, u32[]{:S(2)}) async-start(bf16[16,24,3200]{2,1,0:T(8,128)(2,1)} %bitcast.96), calls=%async_computation | async-start | bytes 4915200 | tf_op jit(solution)/shard_map/all_to_all | solution.py:113
  20.6 1.8 fusion.3
  23.1 1.1 select_reduce_fusion
  24.9 44.6 %all-to-all-done = bf16[16,24,3200]{2,1,0:T(8,128)(2,1)S(1)} async-done(((bf16[16,24,3200]{2,1,0:T(8,128)(2,1)}), bf16[16,24,3200]{2,1,0:T(8,128)(2,1)S(1)}, u32[]{:S(2)}, u32[]{:S(2)}) %all-to-all-start) | async-done | bytes 2457632 | tf_op jit(solution)/shard_map/all_to_all | solution.py:113
  70.9 50.2 %all_gather.12 = bf16[384,1024]{1,0:T(8,128)(2,1)S(1)} all-gather(bf16[24,1024]{1,0:T(8,128)(2,1)S(1)} %convert_element_type.168), channel_id=1, replica_groups=mesh['seq'=16,'col'=2] {'seq'}, dimensions={0}, use_global_device_ids=true | all-gather | bytes 835584 | tf_op jit(solution)/shard_map/all_gather | solution.py:186
  121.1 0.6 pad_maximum_fusion.2
  121.8 1.2 reshape.339.q_ref
  123.0 59.6 %shard_map.139 = (f32[72,4,1024]{2,1,0:T(4,128)}, f32[72,1,64]{2,1,0:T(1,128)}, f32[72,1,64]{2,1,0:T(1,128)}) custom-call(s32[72]{0:T(128)} %get-tuple-element.36.owner_ref, s32[72]{0:T(128)} %get-tuple-element.46.count_ref, bf16[96,4,1024]{2,1,0:T(4,128)(2,1)} %reshape.339.q_ref, bf16[72,128,1024]{2,1,0:T(8,128)(2,1)} %k_ref.1, bf16[72,128,1024]{2,1,0:T(8,128)(2,1)} %v_ref.1), custom_call_target="tpu_custom_call" | custom-call | flops 2415919104 | bytes 37748736 | tf_op jit(solution)/shard_map/pallas_call | solution.py:71
  182.6 0.8 copy.199
  183.5 0.8 select_reduce_fusion.2
  184.3 0.8 select_reduce_fusion.1
  185.2 0.9 copy.207
  186.2 0.7 broadcast_in_dim.179
  186.9 1.7 reshape.341
  188.6 2.5 copy_multiply_fusion
  191.1 1.5 convolution_convert_fusion.1
  193.6 1.1 reshape.343
  194.7 3.6 all-to-all-start.1
  199.1 13.5 %all-to-all-done.1 = bf16[16,24,1152]{2,1,0:T(8,128)(2,1)S(1)} async-done(((bf16[16,24,1152]{2,1,0:T(8,128)(2,1)}), bf16[16,24,1152]{2,1,0:T(8,128)(2,1)S(1)}, u32[]{:S(2)}, u32[]{:S(2)}) %all-to-all-start.1) | async-done | bytes 884768 | tf_op jit(solution)/shard_map/all_to_all | solution.py:113
  212.6 0.9 copy-done.3
  214.4 0.7 fusion.16
  215.1 0.8 copy.216
  215.9 1.8 broadcast_in_dim.182
  217.7 1.8 reshape.345
  219.6 0.8 add.145
  220.7 1.3 convert_element_type.178
  222.3 43.6 %all_gather.13 = bf16[384,1024]{1,0:T(8,128)(2,1)S(1)} all-gather(bf16[24,1024]{1,0:T(8,128)(2,1)S(1)} %divide_convert_fusion), channel_id=1, replica_groups=mesh['seq'=16,'col'=2] {'seq'}, dimensions={0}, use_global_device_ids=true | all-gather | bytes 835584 | tf_op jit(solution)/shard_map/all_gather | solution.py:252
  266.7 1.2 collective-permute-done
  268.0 42.7 %all_gather.14 = bf16[192,2304]{0,1:T(8,128)(2,1)S(1)} all-gather(bf16[192,144]{0,1:T(8,128)(2,1)S(1)} %add_convert_fusion.2), channel_id=1, replica_groups=mesh['seq'=16,'col'=2] {'seq'}, dimensions={1}, use_global_device_ids=true | all-gather | bytes 940032 | tf_op jit(solution)/shard_map/all_gather | solution.py:257
  311.7 2.1 collective-permute-done.1
  314.6 0.9 multiply_reduce_fusion
  315.5 12.0 %broadcast_multiply_fusion = f32[384,4,720]{0,2,1:T(8,128)} fusion(f32[384]{0:T(512)S(1)} %add_rsqrt_fusion, bf16[4,2304,720]{1,2,0:T(8,128)(2,1)} %bitcast.118, bf16[192,2304]{0,1:T(8,128)(2,1)S(1)} %get-tuple-element.50, bf16[192,2304]{0,1:T(8,128)(2,1)S(1)} %get-tuple-element.49), kind=kOutput, calls=%fused_computation.18 | convolution fusion | flops 5100724224 | bytes 19465728 | tf_op jit(solution)/shard_map/rc,ecf->ref/dot_general | solution.py:262
  327.5 0.7 select_reduce_fusion.5
  328.2 7.6 %fusion = f32[384,2304]{1,0:T(8,128)S(1)} fusion(bf16[4,360,2304]{2,1,0:T(8,128)(2,1)S(1)} %bitcast.120, f32[384,4]{0,1:T(4,128)S(1)} %select_add_fusion, f32[384,4,720]{0,2,1:T(8,128)} %broadcast_multiply_fusion), kind=kOutput, calls=%fused_computation.1 | convolution fusion | flops 2557550592 | bytes 14604288 | tf_op jit(solution)/shard_map/ref,efd->red/dot_general | solution.py:280
  335.9 1.7 copy-done.4
  337.6 1.3 constant_dynamic-slice_fusion
  339.1 3.7 collective-permute-done.2
  342.8 1.6 add_convert_fusion
  344.5 1.4 copy.225
  345.9 3.7 all-to-all-start.2
  349.6 54.4 %all-gather.2.cloned.1.call-done = bf16[384,2048]{1,0:T(8,128)(2,1)} async-done(((bf16[24,2048]{1,0:T(8,128)(2,1)}), bf16[384,2048]{1,0:T(8,128)(2,1)}) %all-gather.2.cloned.1.call-update) | async-done | bytes 1572880 | tf_op jit(solution)/shard_map/all_gather | solution.py:190
  404.0 2.5 reshape.354
  407.4 1.1 copy.228
  408.5 1.1 copy.229
  410.0 0.8 copy.227
  (127 shorter events, 11.3 us)
Async XLA Ops:
  7.2 258.8 %copy-start = (bf16[1024,144]{0,1:T(8,128)(2,1)S(1)}, bf16[1024,144]{0,1:T(8,128)(2,1)}, u32[]{:S(2)}) copy-start(bf16[1024,144]{0,1:T(8,128)(2,1)} %param.20) | copy-start | bytes 884740
  7.2 2.1 copy-start.7
  9.3 0.9 copy-start.5
  11.8 8.5 %copy-start.10 = (s32[96]{0:T(128)S(1)}, s32[96]{0:T(128)}, u32[]{:S(2)}) copy-start(s32[96]{0:T(128)} %param.16) | copy-start | bytes 1156
  11.8 8.8 %copy-start.8 = (s32[96,128]{1,0:T(8,128)S(1)}, s32[96,128]{1,0:T(8,128)}, u32[]{:S(2)}) copy-start(s32[96,128]{1,0:T(8,128)} %param.15) | copy-start | bytes 147460
  11.8 57.7 %all-to-all-start = ((bf16[16,24,3200]{2,1,0:T(8,128)(2,1)}), bf16[16,24,3200]{2,1,0:T(8,128)(2,1)S(1)}, u32[]{:S(2)}, u32[]{:S(2)}) async-start(bf16[16,24,3200]{2,1,0:T(8,128)(2,1)} %bitcast.96), calls=%async_computation | async-start | bytes 4915200 | tf_op jit(solution)/shard_map/all_to_all | solution.py:113
  194.7 17.8 %all-to-all-start.1 = ((bf16[16,24,1152]{2,1,0:T(8,128)(2,1)}), bf16[16,24,1152]{2,1,0:T(8,128)(2,1)S(1)}, u32[]{:S(2)}, u32[]{:S(2)}) async-start(bf16[16,24,1152]{2,1,0:T(8,128)(2,1)} %reshape.343), calls=%async_computation.1 | async-start | bytes 1769472 | tf_op jit(solution)/shard_map/all_to_all | solution.py:113
  198.4 205.7 %all-gather.2.cloned.1.call-start = ((), (), s32[]{:S(2)}) async-start(), calls=%async_computation.3 | async-start | bytes 1671168 | tf_op jit(solution)/shard_map/all_gather | solution.py:190
  212.6 0.9 copy-start.3
  219.5 2.5 copy-start.2
  222.0 44.5 %copy-start.6 = (bf16[384,144]{1,0:T(8,128)(2,1)S(1)}, bf16[384,144]{1,0:T(8,128)(2,1)}, u32[]{:S(2)}) copy-start(bf16[384,144]{1,0:T(8,128)(2,1)} %copy-done.5) | copy-start | bytes 331780
  266.3 45.1 %copy-start.9 = (s32[4,96,2]{1,2,0:T(2,128)S(1)}, s32[4,96,2]{1,2,0:T(2,128)}, u32[]{:S(2)}) copy-start(s32[4,96,2]{1,2,0:T(2,128)} %param.18) | copy-start | bytes 9220
  266.4 1.4 collective-permute-start
  311.3 2.5 collective-permute-start.1
  314.6 13.6 %slice-start = ((s8[6635520]{0:T(1024)(128)(4,1)}), s8[4194304]{0:T(1024)(128)(4,1)S(1)}, s32[]{:S(2)}) async-start(s8[6635520]{0:T(1024)(128)(4,1)} %bitcast.119), calls=%async_computation.4 | async-start | bytes 8388608
  315.5 12.0 %copy-start.11 = (bf16[2304,8]{0,1:T(8,128)(2,1)S(1)}, bf16[2304,8]{0,1:T(8,128)(2,1)}, u32[]{:S(2)}) copy-start(bf16[2304,8]{0,1:T(8,128)(2,1)} %param.21) | copy-start | bytes 110596
  315.5 12.7 %slice-start.1 = ((s8[6635520]{0:T(1024)(128)(4,1)}), s8[2441216]{0:T(1024)(128)(4,1)S(1)}, s32[]{:S(2)}) async-start(s8[6635520]{0:T(1024)(128)(4,1)} %bitcast.119), calls=%async_computation.5 | async-start | bytes 4882432
  335.8 1.8 copy-start.4
  338.9 3.9 collective-permute-start.2
  345.9 60.6 %all-to-all-start.2 = ((bf16[16,192,144]{1,2,0:T(8,128)(2,1)}), bf16[16,192,144]{1,2,0:T(8,128)(2,1)S(1)}, u32[]{:S(2)}, u32[]{:S(2)}) async-start(bf16[16,192,144]{1,2,0:T(8,128)(2,1)} %bitcast.22), calls=%async_computation.2 | async-start | bytes 2359296 | tf_op jit(solution)/shard_map/all_to_all | solution.py:113
  406.8 2.9 collective-permute-start.3
  407.4 3.4 copy-start.1
Sparse Core Ops, SparseCore 0:
  339.2 64.7 all-gather.1
